TPU v7x, 32 devices: a whole 2x2x4 slice. The times are simulated.
32 devices in a mesh: lon: 8 (over y, x, core), lat: 4 (over z).
Axes of the slice: x: 2, y: 2, z: 4, core: 2. Of those that a mesh axis runs over, the one named last changes fastest.
Arguments:
- ensemble: float32 [8, 4, 80, 32, 256], P('lon', 'lat'), may hold values from -6 to 6
- obs_block: int32 [3, 128], replicated, may hold values from 0 to 31, as said below
- obs_column: int32 [3, 128], replicated, may hold values from 0 to 255
- obs_value: float32 [3, 128], replicated, may hold values from -8 to 8
- obs_error: float32 [3, 128], replicated, may hold values from 0.5 to 2
- loc_mask: int32 [8, 4, 3, 128, 256], P('lon', 'lat'), may hold values from 0 to 1, as said below
Outputs:
- analysis: float32 [8, 4, 80, 32, 256], P('lon', 'lat')
Inputs may be any that keep to these rules, and one draw needn't show every extreme that they name: `obs_block`: observations fall more often on blocks of low index. `loc_mask`: an observation may update only columns of its own block and of blocks at most two blocks away along longitude (cyclically) and latitude; all other blocks have zeros for it.
All inputs are finite; a program needn't handle non-finite values.
Results may differ from a plain program's by a relative error of at most 0.0001.
Values sent between devices are 32-bit elements; how exact they have to be, the bound alone decides.
No kernel may reach another device: no remote copies, remote signals or barrier semaphores. Data moves between devices by JAX's collectives and lax.ppermute only.
A program may use at most 64 MiB of HBM per device.

v0:
```python
import jax
import jax.numpy as jnp
from jax import lax
from jax.sharding import PartitionSpec as P


def solve_rows(whitened, innov_raw):
    count = whitened.shape[0]
    cmat = jnp.eye(count, dtype=jnp.float32) + jnp.dot(
        whitened, whitened.T, precision=lax.Precision.HIGHEST
    )
    chol = jnp.linalg.cholesky(cmat)
    gain_rows = jax.scipy.linalg.cho_solve((chol, True), whitened)
    innov = jax.scipy.linalg.cho_solve((chol, True), innov_raw)
    return (gain_rows, innov)


def body(ensemble, obs_block, obs_column, obs_value, obs_error, loc_mask):
    members = ensemble.shape[2]
    levels = ensemble.shape[3]
    columns = ensemble.shape[4]
    count = obs_block.shape[1]
    scale = 1.0 / jnp.sqrt(jnp.float32(members - 1))
    n_lat = lax.axis_size("lat")
    lat_here = lax.axis_index("lat")
    state = ensemble.reshape(members, levels * columns)
    col_ids = jnp.arange(columns, dtype=jnp.int32)
    for batch in range(obs_block.shape[0]):
        blocks = obs_block[batch]
        pick = obs_column[batch][:, None] == col_ids[None, :]
        surface = state[:, :columns]
        piece = lax.all_gather(surface[None], "lon", axis=0, tiled=True)
        width = piece.shape[0]
        ids = jnp.arange(width, dtype=jnp.int32) * n_lat + lat_here
        select = ((blocks[:, None] == ids[None, :])[:, :, None] & pick[:, None, :]).astype(
            jnp.float32
        )
        row_part = jnp.zeros((count, members), jnp.float32) + jnp.einsum(
            "pkc,kmc->pm", select, piece, precision=lax.Precision.HIGHEST
        )
        obs_ens = lax.psum(row_part, "lat")
        obs_mean = jnp.mean(obs_ens, axis=1)
        errors = obs_error[batch]
        whitened = (obs_ens - obs_mean[:, None]) * scale / errors[:, None]
        innov_raw = (obs_value[batch] - obs_mean) / errors
        gain_rows, innov = solve_rows(whitened, innov_raw)
        coef = jnp.concatenate([-0.5 * gain_rows.T, (innov * scale)[None, :]], axis=0)
        weights = loc_mask[0, 0, batch].astype(jnp.float32)
        mean = jnp.mean(state, axis=0)
        pert = state - mean[None, :]
        proj = jnp.dot(whitened, pert, precision=lax.Precision.HIGHEST)
        proj = (proj.reshape(count, levels, columns) * weights[:, None, :]).reshape(
            count, levels * columns
        )
        incr = jnp.dot(coef, proj, precision=lax.Precision.HIGHEST)
        state = pert + incr[:members] + (mean + incr[members])[None, :]
    return state.reshape(ensemble.shape)


def solution(mesh):
    placed = (
        P("lon", "lat", None, None, None),
        P(),
        P(),
        P(),
        P(),
        P("lon", "lat", None, None, None),
    )
    return jax.shard_map(
        body,
        mesh=mesh,
        in_specs=placed,
        out_specs=P("lon", "lat", None, None, None),
        check_vma=False,
    )
```

profile of v0, /device:TPU:0, one launch (start us, length us, event | category | flops | bytes accessed | tf_op | source)
XLA Modules:
  0.0 211.4 jit_solution(10639633567476785206)
XLA Ops:
  0.9 3.4 %copy.32 = f32[10,8,32,256]{3,1,2,0:T(8,128)S(1)} copy(f32[10,8,32,256]{3,2,1,0:T(8,128)} %bitcast.215) | data formatting | bytes 5242880
  4.3 11.6 %all-gather = f32[640,256]{1,0:T(8,128)S(1)} all-gather(f32[80,256]{1,0:T(8,128)S(1)} %slice.116), channel_id=2, replica_groups=mesh['lon'=8,'lat'=4] {'lon'}, dimensions={0}, use_global_device_ids=true | all-gather | bytes 737280 | tf_op jit(solution)/shard_map/all_gather | solution.py:32
  16.8 19.8 %psum.21 = f32[128,80]{0,1:T(8,128)S(1)} all-reduce(f32[128,80]{0,1:T(8,128)S(1)} %convolution_bitcast_fusion.2), channel_id=1, replica_groups=mesh['lon'=8,'lat'=4] {'lat'}, use_global_device_ids=true, to_apply=%region_1.0 | all-reduce | flops 10240 | bytes 81920 | tf_op jit(solution)/shard_map/psum | solution.py:41
  37.1 11.7 %cholesky.59 = f32[128,128]{1,0:T(8,128)S(1)} custom-call(f32[128,128]{1,0:T(8,128)S(1)} %fusion.63), custom_call_target="Cholesky" | custom-call | tf_op jit(solution)/shard_map/jit(cholesky)/cholesky | solution.py:12
  50.1 9.8 %custom-call.16 = f32[1,128,128]{1,2,0:T(8,128)S(1)} custom-call(f32[1,128,128]{2,1,0:T(8,128)S(1)} %fusion.31), custom_call_target="InvertDiagBlocksLowerTriangular" | custom-call | tf_op jit(solution)/shard_map/jit(_cho_solve)/triangular_solve | solution.py:13
  61.0 1.9 reduce_sum.54
  64.0 5.1 %fusion.8 = f32[128,32,256]{2,0,1:T(8,128)} fusion(f32[10,32,8,256]{3,2,1,0:T(8,128)S(1)} %bitcast.216, f32[128,256]{1,0:T(8,128)S(1)} %get-tuple-element.13, f32[128,80]{0,1:T(8,128)S(1)} %psum.21, f32[128]{0:T(128)S(1)} %get-tuple-element.18, f32[128]{0:T(128)S(1)} %broadcast_multiply_fusion.4), kind=kOutput, calls=%fused_computation.13 | convolution fusion | flops 1007712256 | bytes 6988800 | tf_op jit(solution)/shard_map/dot_general | solution.py:51
  69.1 5.6 %copy.21 = f32[128,32,256]{0,2,1:T(8,128)} copy(f32[128,32,256]{2,0,1:T(8,128)} %fusion.8) | data formatting | bytes 8388608 | tf_op jit(solution)/shard_map/mul | solution.py:52
  74.7 5.9 %fusion.34 = f32[81,8192]{1,0:T(8,128)S(1)} fusion(f32[128,8192]{0,1:T(8,128)} %bitcast.210, f32[1,128]{0,1:T(8,128)S(1)} %copy.19, f32[80,128]{0,1:T(8,128)S(1)} %fusion.15), kind=kOutput, calls=%fused_computation.62 | convolution fusion | flops 1019226240 | bytes 6889984 | tf_op jit(solution)/shard_map/dot_general | solution.py:55
  82.6 10.1 %all-gather.1 = f32[640,256]{1,0:T(8,128)S(1)} all-gather(f32[80,256]{1,0:T(8,128)S(1)} %slice.119), channel_id=3, replica_groups=mesh['lon'=8,'lat'=4] {'lon'}, dimensions={0}, use_global_device_ids=true | all-gather | bytes 737280 | tf_op jit(solution)/shard_map/all_gather | solution.py:32
  93.6 16.3 %psum.22 = f32[128,80]{0,1:T(8,128)S(1)} all-reduce(f32[128,80]{0,1:T(8,128)S(1)} %convolution_bitcast_fusion.1), channel_id=1, replica_groups=mesh['lon'=8,'lat'=4] {'lat'}, use_global_device_ids=true, to_apply=%region_6.0 | all-reduce | flops 10240 | bytes 81920 | tf_op jit(solution)/shard_map/psum | solution.py:41
  110.3 11.7 %cholesky.70 = f32[128,128]{1,0:T(8,128)S(1)} custom-call(f32[128,128]{1,0:T(8,128)S(1)} %fusion.57), custom_call_target="Cholesky" | custom-call | tf_op jit(solution)/shard_map/jit(cholesky)/cholesky | solution.py:12
  123.5 9.8 %custom-call.18 = f32[1,128,128]{1,2,0:T(8,128)S(1)} custom-call(f32[1,128,128]{2,1,0:T(8,128)S(1)} %fusion.32), custom_call_target="InvertDiagBlocksLowerTriangular" | custom-call | tf_op jit(solution)/shard_map/jit(_cho_solve)/triangular_solve | solution.py:13
  134.7 3.3 %copy.35 = f32[16,8,32,256]{3,1,2,0:T(8,128)S(1)} copy(f32[16,8,32,256]{3,2,1,0:T(8,128)S(1)} %bitcast.213) | data formatting | bytes 8388608
  138.1 4.0 %convolution_multiply_fusion.1 = f32[128,8192]{1,0:T(8,128)S(1)} fusion(f32[128,8192]{1,0:T(8,128)S(1)} %bitcast.211, f32[80,8192]{1,0:T(8,128)S(1)} %copy-done.1, f32[8192]{0:T(1024)S(1)} %broadcast_multiply_fusion.1, f32[128,80]{0,1:T(8,128)S(1)} %psum.22, f32[128]{0:T(128)S(1)} %get-tuple-element.19, f32[128]{0:T(128)S(1)} %broadcast_multiply_fusion.3), kind=kOutput, calls=%fused_computation.1 | convolution fusion | flops 1008367616 | bytes 11084800 | tf_op jit(solution)/shard_map/dot_general | solution.py:51
  142.0 3.0 %fusion.38 = f32[81,8192]{1,0:T(8,128)S(1)} fusion(f32[128,8192]{1,0:T(8,128)S(1)} %convolution_multiply_fusion.1, f32[1,128]{0,1:T(8,128)S(1)} %copy.24, f32[80,128]{0,1:T(8,128)S(1)} %fusion.14), kind=kOutput, calls=%fused_computation.66 | convolution fusion | flops 1019226240 | bytes 6889984 | tf_op jit(solution)/shard_map/dot_general | solution.py:55
  145.6 9.2 %all-gather.2 = f32[640,256]{1,0:T(8,128)S(1)} all-gather(f32[80,256]{1,0:T(8,128)S(1)} %slice.122), channel_id=4, replica_groups=mesh['lon'=8,'lat'=4] {'lon'}, dimensions={0}, use_global_device_ids=true | all-gather | bytes 737280 | tf_op jit(solution)/shard_map/all_gather | solution.py:32
  155.6 18.1 %psum.23 = f32[128,80]{0,1:T(8,128)S(1)} all-reduce(f32[128,80]{0,1:T(8,128)S(1)} %convolution_bitcast_fusion), channel_id=1, replica_groups=mesh['lon'=8,'lat'=4] {'lat'}, use_global_device_ids=true, to_apply=%region_9.13 | all-reduce | flops 10240 | bytes 81920 | tf_op jit(solution)/shard_map/psum | solution.py:41
  174.2 11.7 %cholesky.81 = f32[128,128]{1,0:T(8,128)S(1)} custom-call(f32[128,128]{1,0:T(8,128)S(1)} %fusion.51), custom_call_target="Cholesky" | custom-call | tf_op jit(solution)/shard_map/jit(cholesky)/cholesky | solution.py:12
  187.2 9.8 %custom-call.20 = f32[1,128,128]{1,2,0:T(8,128)S(1)} custom-call(f32[1,128,128]{2,1,0:T(8,128)S(1)} %fusion.33), custom_call_target="InvertDiagBlocksLowerTriangular" | custom-call | tf_op jit(solution)/shard_map/jit(_cho_solve)/triangular_solve | solution.py:13
  198.4 3.3 %copy.36 = f32[16,8,32,256]{3,1,2,0:T(8,128)S(1)} copy(f32[16,8,32,256]{3,2,1,0:T(8,128)S(1)} %bitcast.214) | data formatting | bytes 8388608
  201.7 3.8 %convolution_multiply_fusion = f32[128,8192]{1,0:T(8,128)S(1)} fusion(f32[128,8192]{1,0:T(8,128)S(1)} %bitcast.212, f32[80,8192]{1,0:T(8,128)S(1)} %get-tuple-element.8, f32[8192]{0:T(1024)S(1)} %broadcast_multiply_fusion, f32[128,80]{0,1:T(8,128)S(1)} %psum.23, f32[128]{0:T(128)S(1)} %get-tuple-element.17, f32[128]{0:T(128)S(1)} %broadcast_multiply_fusion.2), kind=kOutput, calls=%fused_computation | convolution fusion | flops 1008367616 | bytes 11084800 | tf_op jit(solution)/shard_map/dot_general | solution.py:51
  205.5 3.0 %fusion.42 = f32[81,8192]{1,0:T(8,128)S(1)} fusion(f32[128,8192]{1,0:T(8,128)S(1)} %convolution_multiply_fusion, f32[1,128]{0,1:T(8,128)S(1)} %copy.27, f32[80,128]{0,1:T(8,128)S(1)} %fusion.13), kind=kOutput, calls=%fused_computation.70 | convolution fusion | flops 1019226240 | bytes 6889984 | tf_op jit(solution)/shard_map/dot_general | solution.py:55
  208.9 2.3 %copy.37 = f32[10,8,32,256]{3,2,1,0:T(8,128)} copy(f32[10,8,32,256]{3,1,2,0:T(8,128)S(1)} %bitcast.217) | data formatting | bytes 5242880
  (80 shorter events, 16.4 us)
Async XLA Ops:
  0.9 15.1 %copy-start.5 = (s32[3,128]{1,0:T(4,128)S(1)}, s32[3,128]{1,0:T(4,128)}, u32[]{:S(2)}) copy-start(s32[3,128]{1,0:T(4,128)} %param.13) | copy-start | bytes 4612
  0.9 35.8 %copy-start.3 = (f32[3,128]{1,0:T(4,128)S(1)}, f32[3,128]{1,0:T(4,128)}, u32[]{:S(2)}) copy-start(f32[3,128]{1,0:T(4,128)} %param.15) | copy-start | bytes 4612
  4.3 56.2 %copy-start.4 = (f32[3,128]{1,0:T(4,128)S(1)}, f32[3,128]{1,0:T(4,128)}, u32[]{:S(2)}) copy-start(f32[3,128]{1,0:T(4,128)} %param.14) | copy-start | bytes 4612
  62.9 1.0 copy-start.2
  81.1 1.5 copy-start
  134.7 3.4 %copy-start.1 = (f32[80,8192]{1,0:T(8,128)S(1)}, f32[80,8192]{1,0:T(8,128)}, u32[]{:S(2)}) copy-start(f32[80,8192]{1,0:T(8,128)} %copy-done) | copy-start | bytes 7864324
where the time goes:
time: 215 us; the launch traced here: 211 us
  blocking collectives  85.1 us (40%)
  other arithmetic  72.7 us (34%)
  matrix products  30.5 us (14%)
  local copies, waits for them, and re-layouts  22.4 us (10%)
    psum x3, blocking collectives, body(): obs_ens = lax.psum(row_part, 'lat')  54.3 us
    another operation x9, other arithmetic, solve_rows(): chol = jnp.linalg.cholesky(cmat)  37.2 us
    another operation x6, other arithmetic, solve_rows(): gain_rows = jax.scipy.linalg.cho_solve((chol, True), whitened)  31.4 us
    all_gather x3, blocking collectives, body(): piece = lax.all_gather(surface[None], 'lon', axis=0, tiled=True)  30.9 us
    unnamed x18, local copies, waits for them, and re-layouts  14.6 us
    dot_general x3, matrix products, body(): proj = jnp.dot(whitened, pert, precision=lax.Precision.HIGHEST)  12.9 us
    dot_general x3, matrix products, body(): incr = jnp.dot(coef, proj, precision=lax.Precision.HIGHEST)  12 us
    mul x3, local copies, waits for them, and re-layouts, body(): proj.reshape(count, levels, columns) * weights[:, None, :]  6.22 us

commit v1 on v0

--- a/solution.py
+++ b/solution.py
@@ -38,7 +38,8 @@
         row_part = jnp.zeros((count, members), jnp.float32) + jnp.einsum(
             "pkc,kmc->pm", select, piece, precision=lax.Precision.HIGHEST
         )
-        obs_ens = lax.psum(row_part, "lat")
+        parts = lax.all_gather(row_part, "lat")
+        obs_ens = jnp.sum(parts, axis=0)
         obs_mean = jnp.mean(obs_ens, axis=1)
         errors = obs_error[batch]
         whitened = (obs_ens - obs_mean[:, None]) * scale / errors[:, None]

time: 215 us -> 201 us (0.935)
  blocking collectives: 85.1 us -> 72.4 us
    psum x3 -> x0, blocking collectives: 54.3 us -> none  [body(): obs_ens = lax.psum(row_part, 'lat')]
    all_gather x0 -> x3, blocking collectives: none -> 41.5 us  [body(): parts = lax.all_gather(row_part, 'lat')]
where the time goes in v1:
time: 201 us; the launch traced here: 198 us
  other arithmetic  73.1 us (36%)
  blocking collectives  72.4 us (36%)
  matrix products  29.6 us (15%)
  local copies, waits for them, and re-layouts  22.1 us (11%)
    all_gather x3, blocking collectives, body(): parts = lax.all_gather(row_part, 'lat')  41.5 us
    another operation x9, other arithmetic, solve_rows(): chol = jnp.linalg.cholesky(cmat)  37.2 us
    another operation x6, other arithmetic, solve_rows(): gain_rows = jax.scipy.linalg.cho_solve((chol, True), whitened)  31.4 us
    all_gather x3, blocking collectives, body(): piece = lax.all_gather(surface[None], 'lon', axis=0, tiled=True)  30.8 us
    unnamed x18, local copies, waits for them, and re-layouts  14.6 us
    dot_general x3, matrix products, body(): proj = jnp.dot(whitened, pert, precision=lax.Precision.HIGHEST)  12.6 us
    dot_general x3, matrix products, body(): incr = jnp.dot(coef, proj, precision=lax.Precision.HIGHEST)  11.5 us
    mul x3, local copies, waits for them, and re-layouts, body(): proj.reshape(count, levels, columns) * weights[:, None, :]  6.24 us

profile of v1, /device:TPU:0, one launch (start us, length us, event | category | flops | bytes accessed | tf_op | source)
XLA Modules:
  0.0 198.0 jit_solution(7807502004893553199)
XLA Ops:
  0.9 3.4 %copy.40 = f32[10,8,32,256]{3,1,2,0:T(8,128)S(1)} copy(f32[10,8,32,256]{3,2,1,0:T(8,128)} %bitcast.227) | data formatting | bytes 5242880
  4.3 11.6 %all-gather = f32[640,256]{1,0:T(8,128)S(1)} all-gather(f32[80,256]{1,0:T(8,128)S(1)} %slice.116), channel_id=2, replica_groups=mesh['lon'=8,'lat'=4] {'lon'}, dimensions={0}, use_global_device_ids=true | all-gather | bytes 737280 | tf_op jit(solution)/shard_map/all_gather | solution.py:32
  16.8 13.9 %all-gather.1 = f32[512,80]{0,1:T(8,128)S(1)} all-gather(f32[128,80]{0,1:T(8,128)S(1)} %convolution_bitcast_fusion.2), channel_id=3, replica_groups=mesh['lon'=8,'lat'=4] {'lat'}, dimensions={0}, use_global_device_ids=true | all-gather | bytes 204800 | tf_op jit(solution)/shard_map/all_gather | solution.py:41
  31.3 11.7 %cholesky.59 = f32[128,128]{1,0:T(8,128)S(1)} custom-call(f32[128,128]{1,0:T(8,128)S(1)} %fusion.51), custom_call_target="Cholesky" | custom-call | tf_op jit(solution)/shard_map/jit(cholesky)/cholesky | solution.py:12
  44.4 9.8 %custom-call.16 = f32[1,128,128]{1,2,0:T(8,128)S(1)} custom-call(f32[1,128,128]{2,1,0:T(8,128)S(1)} %fusion.31), custom_call_target="InvertDiagBlocksLowerTriangular" | custom-call | tf_op jit(solution)/shard_map/jit(_cho_solve)/triangular_solve | solution.py:13
  55.0 2.0 reduce_sum.81
  58.0 5.1 %fusion.8 = f32[128,32,256]{2,0,1:T(8,128)} fusion(f32[10,32,8,256]{3,2,1,0:T(8,128)S(1)} %bitcast.228, f32[128,256]{1,0:T(8,128)S(1)} %get-tuple-element.13, f32[128,80]{0,1:T(8,128)S(1)} %reduce_sum.82, f32[128]{0:T(128)S(1)} %get-tuple-element.18, f32[128]{0:T(128)S(1)} %broadcast_multiply_fusion.4), kind=kOutput, calls=%fused_computation.13 | convolution fusion | flops 1007712256 | bytes 6988800 | tf_op jit(solution)/shard_map/dot_general | solution.py:52
  63.2 5.6 %copy.31 = f32[128,32,256]{0,2,1:T(8,128)} copy(f32[128,32,256]{2,0,1:T(8,128)} %fusion.8) | data formatting | bytes 8388608 | tf_op jit(solution)/shard_map/mul | solution.py:53
  68.7 6.2 %fusion.52 = f32[81,8192]{1,0:T(8,128)S(1)} fusion(f32[128,8192]{0,1:T(8,128)} %bitcast.224, f32[1,128]{1,0:T(1,128)S(1)} %fusion.21, f32[80,128]{1,0:T(8,128)S(1)} %fusion.15), kind=kOutput, calls=%fused_computation.89 | convolution fusion | flops 1019226240 | bytes 6889984 | tf_op jit(solution)/shard_map/dot_general | solution.py:56
  77.0 10.1 %all-gather.2 = f32[640,256]{1,0:T(8,128)S(1)} all-gather(f32[80,256]{1,0:T(8,128)S(1)} %slice.119), channel_id=4, replica_groups=mesh['lon'=8,'lat'=4] {'lon'}, dimensions={0}, use_global_device_ids=true | all-gather | bytes 737280 | tf_op jit(solution)/shard_map/all_gather | solution.py:32
  88.0 13.9 %all-gather.3 = f32[512,80]{0,1:T(8,128)S(1)} all-gather(f32[128,80]{0,1:T(8,128)S(1)} %convolution_bitcast_fusion.1), channel_id=5, replica_groups=mesh['lon'=8,'lat'=4] {'lat'}, dimensions={0}, use_global_device_ids=true | all-gather | bytes 204800 | tf_op jit(solution)/shard_map/all_gather | solution.py:41
  102.5 11.7 %cholesky.70 = f32[128,128]{1,0:T(8,128)S(1)} custom-call(f32[128,128]{1,0:T(8,128)S(1)} %fusion.45), custom_call_target="Cholesky" | custom-call | tf_op jit(solution)/shard_map/jit(cholesky)/cholesky | solution.py:12
  115.7 9.8 %custom-call.18 = f32[1,128,128]{1,2,0:T(8,128)S(1)} custom-call(f32[1,128,128]{2,1,0:T(8,128)S(1)} %fusion.32), custom_call_target="InvertDiagBlocksLowerTriangular" | custom-call | tf_op jit(solution)/shard_map/jit(_cho_solve)/triangular_solve | solution.py:13
  126.7 3.3 %copy.43 = f32[16,8,32,256]{3,1,2,0:T(8,128)S(1)} copy(f32[16,8,32,256]{3,2,1,0:T(8,128)S(1)} %bitcast.225) | data formatting | bytes 8388608
  130.0 3.7 %convolution_multiply_fusion.1 = f32[128,8192]{1,0:T(8,128)S(1)} fusion(f32[128,8192]{1,0:T(8,128)S(1)} %bitcast.222, f32[80,8192]{1,0:T(8,128)S(1)} %copy-done.1, f32[8192]{0:T(1024)S(1)} %broadcast_multiply_fusion.1, f32[128,80]{0,1:T(8,128)S(1)} %reduce_sum.85, f32[128]{0:T(128)S(1)} %get-tuple-element.19, f32[128]{0:T(128)S(1)} %broadcast_multiply_fusion.3), kind=kOutput, calls=%fused_computation.1 | convolution fusion | flops 1008367616 | bytes 11084800 | tf_op jit(solution)/shard_map/dot_general | solution.py:52
  133.8 2.6 %fusion.56 = f32[81,8192]{1,0:T(8,128)S(1)} fusion(f32[128,8192]{1,0:T(8,128)S(1)} %convolution_multiply_fusion.1, f32[1,128]{1,0:T(1,128)S(1)} %fusion.19, f32[80,128]{1,0:T(8,128)S(1)} %fusion.14), kind=kOutput, calls=%fused_computation.93 | convolution fusion | flops 1019226240 | bytes 6889984 | tf_op jit(solution)/shard_map/dot_general | solution.py:56
  136.9 9.1 %all-gather.4 = f32[640,256]{1,0:T(8,128)S(1)} all-gather(f32[80,256]{1,0:T(8,128)S(1)} %slice.122), channel_id=6, replica_groups=mesh['lon'=8,'lat'=4] {'lon'}, dimensions={0}, use_global_device_ids=true | all-gather | bytes 737280 | tf_op jit(solution)/shard_map/all_gather | solution.py:32
  146.9 13.8 %all-gather.5 = f32[512,80]{0,1:T(8,128)S(1)} all-gather(f32[128,80]{0,1:T(8,128)S(1)} %convolution_bitcast_fusion), channel_id=7, replica_groups=mesh['lon'=8,'lat'=4] {'lat'}, dimensions={0}, use_global_device_ids=true | all-gather | bytes 204800 | tf_op jit(solution)/shard_map/all_gather | solution.py:41
  161.3 11.7 %cholesky.81 = f32[128,128]{1,0:T(8,128)S(1)} custom-call(f32[128,128]{1,0:T(8,128)S(1)} %fusion.39), custom_call_target="Cholesky" | custom-call | tf_op jit(solution)/shard_map/jit(cholesky)/cholesky | solution.py:12
  174.4 9.8 %custom-call.20 = f32[1,128,128]{1,2,0:T(8,128)S(1)} custom-call(f32[1,128,128]{2,1,0:T(8,128)S(1)} %fusion.33), custom_call_target="InvertDiagBlocksLowerTriangular" | custom-call | tf_op jit(solution)/shard_map/jit(_cho_solve)/triangular_solve | solution.py:13
  185.4 3.3 %copy.44 = f32[16,8,32,256]{3,1,2,0:T(8,128)S(1)} copy(f32[16,8,32,256]{3,2,1,0:T(8,128)S(1)} %bitcast.226) | data formatting | bytes 8388608
  188.7 3.8 %convolution_multiply_fusion = f32[128,8192]{1,0:T(8,128)S(1)} fusion(f32[128,8192]{1,0:T(8,128)S(1)} %bitcast.223, f32[80,8192]{1,0:T(8,128)S(1)} %get-tuple-element.8, f32[8192]{0:T(1024)S(1)} %broadcast_multiply_fusion, f32[128,80]{0,1:T(8,128)S(1)} %reduce_sum.88, f32[128]{0:T(128)S(1)} %get-tuple-element.17, f32[128]{0:T(128)S(1)} %broadcast_multiply_fusion.2), kind=kOutput, calls=%fused_computation | convolution fusion | flops 1008367616 | bytes 11084800 | tf_op jit(solution)/shard_map/dot_general | solution.py:52
  192.5 2.6 %fusion.60 = f32[81,8192]{1,0:T(8,128)S(1)} fusion(f32[128,8192]{1,0:T(8,128)S(1)} %convolution_multiply_fusion, f32[1,128]{1,0:T(1,128)S(1)} %fusion.17, f32[80,128]{1,0:T(8,128)S(1)} %fusion.13), kind=kOutput, calls=%fused_computation.97 | convolution fusion | flops 1019226240 | bytes 6889984 | tf_op jit(solution)/shard_map/dot_general | solution.py:56
  195.4 2.3 %copy.45 = f32[10,8,32,256]{3,2,1,0:T(8,128)} copy(f32[10,8,32,256]{3,1,2,0:T(8,128)S(1)} %bitcast.229) | data formatting | bytes 5242880
  (86 shorter events, 16.3 us)
Async XLA Ops:
  0.9 15.1 %copy-start.5 = (s32[3,128]{1,0:T(4,128)S(1)}, s32[3,128]{1,0:T(4,128)}, u32[]{:S(2)}) copy-start(s32[3,128]{1,0:T(4,128)} %param.13) | copy-start | bytes 4612
  0.9 30.0 %copy-start.3 = (f32[3,128]{1,0:T(4,128)S(1)}, f32[3,128]{1,0:T(4,128)}, u32[]{:S(2)}) copy-start(f32[3,128]{1,0:T(4,128)} %param.15) | copy-start | bytes 4612
  4.3 50.3 %copy-start.4 = (f32[3,128]{1,0:T(4,128)S(1)}, f32[3,128]{1,0:T(4,128)}, u32[]{:S(2)}) copy-start(f32[3,128]{1,0:T(4,128)} %param.14) | copy-start | bytes 4612
  57.0 1.0 copy-start.2
  75.5 1.5 copy-start
  126.7 3.4 %copy-start.1 = (f32[80,8192]{1,0:T(8,128)S(1)}, f32[80,8192]{1,0:T(8,128)}, u32[]{:S(2)}) copy-start(f32[80,8192]{1,0:T(8,128)} %copy-done) | copy-start | bytes 7864324
